TPU v7x, 32 devices: a whole 2x2x4 slice. The times are simulated.
32 devices in a mesh: dp: 8 (over z, y), fsdp: 4 (over x, core).
Axes of the slice: x: 2, y: 2, z: 4, core: 2. Of those that a mesh axis runs over, the one named last changes fastest.
Arguments:
- tokens: bfloat16 [2, 8192, 1152], P(None, ('dp', 'fsdp')), may hold values from -6 to 6
- condition: bfloat16 [2, 32, 2, 1152], P(None, ('dp', 'fsdp')), may hold values from -6 to 6
- lengths: int32 [2, 32, 2], P(None, ('dp', 'fsdp')), may hold values from 0 to 256, as said below
- w_mod: bfloat16 [1152, 6912], P('fsdp'), may hold values from -0.1875 to 0.1875
- b_mod: float32 [6912], replicated, may hold values from -1.75 to 1.75
- w_qkv: bfloat16 [1152, 3456], P('fsdp'), may hold values from -0.1875 to 0.1875
- b_qkv: float32 [3456], replicated, may hold values from -1.75 to 1.75
- q_gain: float32 [72], replicated, may hold values from 1 to 1.8
- k_gain: float32 [72], replicated, may hold values from 1 to 1.8
- w_o: bfloat16 [1152, 1152], P('fsdp'), may hold values from -0.75 to 0.75
- b_o: float32 [1152], replicated, may hold values from -1.75 to 1.75
- w_gate: bfloat16 [1152, 3072], P('fsdp'), may hold values from -0.1875 to 0.1875
- w_up: bfloat16 [1152, 3072], P('fsdp'), may hold values from -0.1875 to 0.1875
- w_down: bfloat16 [3072, 1152], P('fsdp'), may hold values from -0.109375 to 0.109375
- d_out: bfloat16 [2, 8192, 1152], P(None, ('dp', 'fsdp')), may hold values from -6 to 6
Outputs:
- block_out: bfloat16 [2, 8192, 1152], P(None, ('dp', 'fsdp'))
- d_tokens: float32 [2, 8192, 1152], P(None, ('dp', 'fsdp'))
- d_condition: float32 [2, 32, 2, 1152], P(None, ('dp', 'fsdp'))
- g_mod: float32 [1152, 6912], P('fsdp')
- g_bmod: float32 [6912], replicated
- g_qkv: float32 [1152, 3456], P('fsdp')
- g_bqkv: float32 [3456], replicated
- g_qgain: float32 [72], replicated
- g_kgain: float32 [72], replicated
- g_o: float32 [1152, 1152], P('fsdp')
- g_bo: float32 [1152], replicated
- g_gate: float32 [1152, 3072], P('fsdp')
- g_up: float32 [1152, 3072], P('fsdp')
- g_down: float32 [3072, 1152], P('fsdp')
Inputs may be any that keep to these rules, and one draw needn't show every extreme that they name: `lengths`: each packed row of 256 tokens holds either one image of 256 patches in slot 0 (slot 1 empty, length 0) or two images of 128 patches; every image has 16 rows of patches; the first row of every micro-batch holds one image.
All inputs are finite; a program needn't handle non-finite values.
Results may differ from a plain program's by a relative error of at most 0.019.
Values may be sent and summed in bfloat16 or wider, within the bound.
No kernel may reach another device: no remote copies, remote signals or barrier semaphores. Data moves between devices by JAX's collectives and lax.ppermute only.
A program may use at most 320 MiB of HBM per device.

v0:
```python
from functools import partial
import jax
import jax.numpy as jnp
from jax import lax
from jax.sharding import PartitionSpec as P

GRID_H = 16
EPSILON = 1e-06
MASKED = -1e30


def silu_grad(values):
    sigmoid = jax.nn.sigmoid(values)
    return sigmoid * (1.0 + values * (1.0 - sigmoid))


def pack_layout(lengths_row, row_count):
    slot_count = lengths_row.shape[0]
    slot_ends = jnp.cumsum(lengths_row)
    slot_starts = slot_ends - lengths_row
    tok_index = jnp.arange(row_count, dtype=jnp.int32)
    segment = jnp.sum(
        (tok_index[:, None] >= slot_ends[None, : slot_count - 1]).astype(jnp.int32), axis=1
    )
    slot_ids = jnp.arange(slot_count, dtype=jnp.int32)
    member = segment[:, None] == slot_ids[None, :]
    offset = jnp.sum(jnp.where(member, slot_starts[None, :], 0), axis=1)
    widths = jnp.maximum(lengths_row // GRID_H, 1)
    tok_width = jnp.sum(jnp.where(member, widths[None, :], 0), axis=1)
    position = tok_index - offset
    return (segment, member.astype(jnp.float32), position // tok_width, position % tok_width)


def rope_angles(grid_row, grid_col, head_dim):
    quarter = head_dim // 4
    frequency = 10000.0 ** (-jnp.arange(quarter, dtype=jnp.float32) / quarter)
    angle_table = jnp.concatenate(
        [
            grid_row.astype(jnp.float32)[:, None] * frequency[None, :],
            grid_col.astype(jnp.float32)[:, None] * frequency[None, :],
        ],
        axis=1,
    )
    return (jnp.cos(angle_table)[:, None, :], jnp.sin(angle_table)[:, None, :])


def norm_mod(field, scale_part, shift_part):
    inverse = lax.rsqrt(jnp.mean(field * field, axis=-1, keepdims=True) + EPSILON)
    return field * inverse * (1.0 + scale_part) + shift_part


def rotate(vector, cosine, sine_table):
    half_dim = vector.shape[-1] // 2
    first = vector[..., :half_dim]
    second = vector[..., half_dim:]
    return jnp.concatenate(
        [first * cosine - second * sine_table, second * cosine + first * sine_table], axis=-1
    )


def head_prep(cosine, sine_table, raw_head, gain_vec):
    inverse = lax.rsqrt(jnp.mean(raw_head * raw_head, axis=-1, keepdims=True) + EPSILON)
    return rotate(raw_head * inverse * gain_vec, cosine, sine_table)


def score_block(q_rot, k_rot, same_slot, score_scale):
    raw_score = jnp.einsum("qhd,khd->hqk", q_rot, k_rot, preferred_element_type=jnp.float32)
    return jnp.where(same_slot[None, :, :], raw_score * score_scale, MASKED)


def forward(row_tokens, row_cond, row_lengths, matrices, minor_params):
    w_mod, w_qkv, w_o, w_gate, w_up, w_down = matrices
    b_mod, b_qkv, q_gain, k_gain, b_o = minor_params
    row_count, model_width = row_tokens.shape
    head_dim = q_gain.shape[0]
    head_count = model_width // head_dim
    segment, member, grid_row, grid_col = pack_layout(row_lengths, row_count)
    cosine, sine_table = rope_angles(grid_row, grid_col, head_dim)
    cond_float = row_cond.astype(jnp.float32)
    silu_cond = jax.nn.silu(cond_float).astype(jnp.bfloat16)
    mod_slots = jnp.dot(silu_cond, w_mod, preferred_element_type=jnp.float32) + b_mod
    mod_tokens = jnp.dot(member, mod_slots, precision=lax.Precision.HIGHEST)
    mod_parts = [
        mod_tokens[:, slot_part * model_width : (slot_part + 1) * model_width]
        for slot_part in range(6)
    ]
    tok_float = row_tokens.astype(jnp.float32)
    norm_one = norm_mod(tok_float, mod_parts[1], mod_parts[0]).astype(jnp.bfloat16)
    qkv_all = jnp.dot(norm_one, w_qkv, preferred_element_type=jnp.float32) + b_qkv
    q_raw = qkv_all[:, :model_width].reshape(row_count, head_count, head_dim)
    k_raw = qkv_all[:, model_width : 2 * model_width].reshape(row_count, head_count, head_dim)
    v_low = (
        qkv_all[:, 2 * model_width :].reshape(row_count, head_count, head_dim).astype(jnp.bfloat16)
    )
    q_rot = head_prep(cosine, sine_table, q_raw, q_gain).astype(jnp.bfloat16)
    k_rot = head_prep(cosine, sine_table, k_raw, k_gain).astype(jnp.bfloat16)
    same_slot = segment[:, None] == segment[None, :]
    score_scale = head_dim ** (-0.5)
    score = score_block(q_rot, k_rot, same_slot, score_scale)
    top_score = jnp.max(score, axis=-1, keepdims=True)
    log_total = top_score + jnp.log(jnp.sum(jnp.exp(score - top_score), axis=-1, keepdims=True))
    attn_prob = jnp.exp(score - log_total)
    attn_out = jnp.einsum(
        "hqk,khd->qhd", attn_prob.astype(jnp.bfloat16), v_low, preferred_element_type=jnp.float32
    )
    attn_out = attn_out.astype(jnp.bfloat16).reshape(row_count, model_width)
    branch = jnp.dot(attn_out, w_o, preferred_element_type=jnp.float32) + b_o
    res_one = tok_float + mod_parts[2] * branch
    norm_two = norm_mod(res_one, mod_parts[4], mod_parts[3]).astype(jnp.bfloat16)
    gate_pre = jnp.dot(norm_two, w_gate, preferred_element_type=jnp.float32)
    up_pre = jnp.dot(norm_two, w_up, preferred_element_type=jnp.float32)
    hidden = (jax.nn.silu(gate_pre) * up_pre).astype(jnp.bfloat16)
    mlp_out = jnp.dot(hidden, w_down, preferred_element_type=jnp.float32)
    block_row = res_one + mod_parts[5] * mlp_out
    stored = {
        "member": member,
        "cosine": cosine,
        "sine_table": sine_table,
        "cond_float": cond_float,
        "silu_cond": silu_cond,
        "mod_parts": mod_parts,
        "tok_float": tok_float,
        "norm_one": norm_one,
        "q_raw": q_raw,
        "k_raw": k_raw,
        "q_rot": q_rot,
        "k_rot": k_rot,
        "v_low": v_low,
        "same_slot": same_slot,
        "log_total": log_total,
        "attn_out": attn_out,
        "branch": branch,
        "res_one": res_one,
        "norm_two": norm_two,
        "gate_pre": gate_pre,
        "up_pre": up_pre,
        "hidden": hidden,
        "mlp_out": mlp_out,
    }
    return (block_row, stored)


def backward(stored, row_grad, matrices, minor_params):
    w_mod, w_qkv, w_o, w_gate, w_up, w_down = matrices
    b_mod, b_qkv, q_gain, k_gain, b_o = minor_params
    row_count, model_width = row_grad.shape
    head_dim = q_gain.shape[0]
    head_count = model_width // head_dim
    score_scale = head_dim ** (-0.5)
    mod_parts = stored["mod_parts"]
    d_mlp = (row_grad * mod_parts[5]).astype(jnp.bfloat16)
    d_gate2 = row_grad * stored["mlp_out"]
    g_down = jnp.dot(stored["hidden"].T, d_mlp, preferred_element_type=jnp.float32)
    d_hidden = jnp.dot(d_mlp, w_down.T, preferred_element_type=jnp.float32)
    gate_pre = stored["gate_pre"]
    d_gate = (d_hidden * stored["up_pre"] * silu_grad(gate_pre)).astype(jnp.bfloat16)
    d_upper = (d_hidden * jax.nn.silu(gate_pre)).astype(jnp.bfloat16)
    g_gate = jnp.dot(stored["norm_two"].T, d_gate, preferred_element_type=jnp.float32)
    g_up = jnp.dot(stored["norm_two"].T, d_upper, preferred_element_type=jnp.float32)
    d_norm_two = jnp.dot(d_gate, w_gate.T, preferred_element_type=jnp.float32) + jnp.dot(
        d_upper, w_up.T, preferred_element_type=jnp.float32
    )
    unused_two, back_two = jax.vjp(norm_mod, stored["res_one"], mod_parts[4], mod_parts[3])
    d_res_norm, d_scale2, d_shift2 = back_two(d_norm_two)
    d_res_one = row_grad + d_res_norm
    d_branch = d_res_one * mod_parts[2]
    d_gate1 = d_res_one * stored["branch"]
    g_bo = jnp.sum(d_branch, axis=0)
    d_proj = d_branch.astype(jnp.bfloat16)
    g_o = jnp.dot(stored["attn_out"].T, d_proj, preferred_element_type=jnp.float32)
    d_attn = (
        jnp.dot(d_proj, w_o.T, preferred_element_type=jnp.float32)
        .astype(jnp.bfloat16)
        .reshape(row_count, head_count, head_dim)
    )
    q_rot = stored["q_rot"]
    k_rot = stored["k_rot"]
    v_low = stored["v_low"]
    score = score_block(q_rot, k_rot, stored["same_slot"], score_scale)
    attn_prob = jnp.exp(score - stored["log_total"])
    d_prob = jnp.einsum("qhd,khd->hqk", d_attn, v_low, preferred_element_type=jnp.float32)
    d_value = jnp.einsum(
        "hqk,qhd->khd", attn_prob.astype(jnp.bfloat16), d_attn, preferred_element_type=jnp.float32
    )
    row_dot = jnp.sum(attn_prob * d_prob, axis=-1, keepdims=True)
    d_score = (attn_prob * (d_prob - row_dot) * score_scale).astype(jnp.bfloat16)
    d_q_rot = jnp.einsum("hqk,khd->qhd", d_score, k_rot, preferred_element_type=jnp.float32)
    d_k_rot = jnp.einsum("hqk,qhd->khd", d_score, q_rot, preferred_element_type=jnp.float32)
    prep_fn = partial(head_prep, stored["cosine"], stored["sine_table"])
    unused_q, back_query = jax.vjp(prep_fn, stored["q_raw"], q_gain)
    d_query, g_qgain = back_query(d_q_rot)
    unused_k, back_key = jax.vjp(prep_fn, stored["k_raw"], k_gain)
    d_key, g_kgain = back_key(d_k_rot)
    d_qkv = jnp.concatenate(
        [
            d_query.reshape(row_count, model_width),
            d_key.reshape(row_count, model_width),
            d_value.reshape(row_count, model_width),
        ],
        axis=1,
    )
    g_bqkv = jnp.sum(d_qkv, axis=0)
    d_qkv_low = d_qkv.astype(jnp.bfloat16)
    g_qkv = jnp.dot(stored["norm_one"].T, d_qkv_low, preferred_element_type=jnp.float32)
    d_norm_one = jnp.dot(d_qkv_low, w_qkv.T, preferred_element_type=jnp.float32)
    unused_one, back_one = jax.vjp(norm_mod, stored["tok_float"], mod_parts[1], mod_parts[0])
    d_tok_norm, d_scale1, d_shift1 = back_one(d_norm_one)
    d_tokens = d_res_one + d_tok_norm
    d_mod_tokens = jnp.concatenate(
        [d_shift1, d_scale1, d_gate1, d_shift2, d_scale2, d_gate2], axis=1
    )
    d_mod = jnp.dot(stored["member"].T, d_mod_tokens, precision=lax.Precision.HIGHEST)
    g_bmod = jnp.sum(d_mod, axis=0)
    d_mod_low = d_mod.astype(jnp.bfloat16)
    g_mod = jnp.dot(stored["silu_cond"].T, d_mod_low, preferred_element_type=jnp.float32)
    d_condition = jnp.dot(d_mod_low, w_mod.T, preferred_element_type=jnp.float32) * silu_grad(
        stored["cond_float"]
    )
    return (
        d_tokens,
        d_condition,
        (g_mod, g_qkv, g_o, g_gate, g_up, g_down),
        (g_bmod, g_bqkv, g_qgain, g_kgain, g_bo),
    )


def sum_data(grad_parts):
    return (
        lax.psum(grad_parts[0].astype(jnp.bfloat16), "dp").astype(jnp.float32),
        lax.psum(grad_parts[1].astype(jnp.bfloat16), "dp").astype(jnp.float32),
        lax.psum(grad_parts[2].astype(jnp.bfloat16), "dp").astype(jnp.float32),
        lax.psum(grad_parts[3].astype(jnp.bfloat16), "dp").astype(jnp.float32),
        lax.psum(grad_parts[4].astype(jnp.bfloat16), "dp").astype(jnp.float32),
        lax.psum(grad_parts[5].astype(jnp.bfloat16), "dp").astype(jnp.float32),
    )


def add_parts(first_parts, second_parts):
    return tuple(
        (left_part + right_part for left_part, right_part in zip(first_parts, second_parts))
    )


def shards(
    tokens,
    condition,
    lengths,
    w_mod,
    b_mod,
    w_qkv,
    b_qkv,
    q_gain,
    k_gain,
    w_o,
    b_o,
    w_gate,
    w_up,
    w_down,
    d_out,
):
    minor_params = (b_mod, b_qkv, q_gain, k_gain, b_o)
    micro_count = tokens.shape[0]
    out_rows = []
    grad_rows = []
    cond_rows = []
    shard_total = None
    minor_total = None
    for micro in range(micro_count):
        matrices = (
            lax.all_gather(w_mod, "fsdp", axis=0, tiled=True),
            lax.all_gather(w_qkv, "fsdp", axis=0, tiled=True),
            lax.all_gather(w_o, "fsdp", axis=0, tiled=True),
            lax.all_gather(w_gate, "fsdp", axis=0, tiled=True),
            lax.all_gather(w_up, "fsdp", axis=0, tiled=True),
            lax.all_gather(w_down, "fsdp", axis=0, tiled=True),
        )
        block_row, stored = forward(
            tokens[micro], condition[micro, 0], lengths[micro, 0], matrices, minor_params
        )
        out_rows.append(block_row.astype(jnp.bfloat16))
        back_matrices = (
            lax.all_gather(w_mod, "fsdp", axis=0, tiled=True),
            lax.all_gather(w_qkv, "fsdp", axis=0, tiled=True),
            lax.all_gather(w_o, "fsdp", axis=0, tiled=True),
            lax.all_gather(w_gate, "fsdp", axis=0, tiled=True),
            lax.all_gather(w_up, "fsdp", axis=0, tiled=True),
            lax.all_gather(w_down, "fsdp", axis=0, tiled=True),
        )
        d_row, d_cond_row, full_grads, minor_grads = backward(
            stored, d_out[micro].astype(jnp.float32), back_matrices, minor_params
        )
        grad_rows.append(d_row)
        cond_rows.append(d_cond_row[None, :, :])
        shard_grads = (
            lax.psum_scatter(
                full_grads[0].astype(jnp.bfloat16), "fsdp", scatter_dimension=0, tiled=True
            ).astype(jnp.float32),
            lax.psum_scatter(
                full_grads[1].astype(jnp.bfloat16), "fsdp", scatter_dimension=0, tiled=True
            ).astype(jnp.float32),
            lax.psum_scatter(
                full_grads[2].astype(jnp.bfloat16), "fsdp", scatter_dimension=0, tiled=True
            ).astype(jnp.float32),
            lax.psum_scatter(
                full_grads[3].astype(jnp.bfloat16), "fsdp", scatter_dimension=0, tiled=True
            ).astype(jnp.float32),
            lax.psum_scatter(
                full_grads[4].astype(jnp.bfloat16), "fsdp", scatter_dimension=0, tiled=True
            ).astype(jnp.float32),
            lax.psum_scatter(
                full_grads[5].astype(jnp.bfloat16), "fsdp", scatter_dimension=0, tiled=True
            ).astype(jnp.float32),
        )
        shard_grads = sum_data(shard_grads)
        shard_total = shard_grads if shard_total is None else add_parts(shard_total, shard_grads)
        minor_total = minor_grads if minor_total is None else add_parts(minor_total, minor_grads)
    minor_sums = lax.psum(
        (minor_total[0], minor_total[1], minor_total[2], minor_total[3], minor_total[4]),
        ("dp", "fsdp"),
    )
    block_out = jnp.stack(out_rows, axis=0)
    d_tokens = jnp.stack(grad_rows, axis=0)
    d_condition = jnp.stack(cond_rows, axis=0)
    return (
        block_out,
        d_tokens,
        d_condition,
        shard_total[0],
        minor_sums[0],
        shard_total[1],
        minor_sums[1],
        minor_sums[2],
        minor_sums[3],
        shard_total[2],
        minor_sums[4],
        shard_total[3],
        shard_total[4],
        shard_total[5],
    )


def solution(mesh):
    placed = (
        P(None, ("dp", "fsdp"), None),
        P(None, ("dp", "fsdp"), None, None),
        P(None, ("dp", "fsdp"), None),
        P("fsdp", None),
        P(),
        P("fsdp", None),
        P(),
        P(),
        P(),
        P("fsdp", None),
        P(),
        P("fsdp", None),
        P("fsdp", None),
        P("fsdp", None),
        P(None, ("dp", "fsdp"), None),
    )
    return jax.shard_map(
        shards,
        mesh=mesh,
        in_specs=placed,
        out_specs=(
            P(None, ("dp", "fsdp"), None),
            P(None, ("dp", "fsdp"), None),
            P(None, ("dp", "fsdp"), None, None),
            P("fsdp", None),
            P(),
            P("fsdp", None),
            P(),
            P(),
            P(),
            P("fsdp", None),
            P(),
            P("fsdp", None),
            P("fsdp", None),
            P("fsdp", None),
        ),
        check_vma=False,
    )
```

profile of v0, /device:TPU:0, one launch (start us, length us, event | category | flops | bytes accessed | tf_op | source)
XLA Modules:
  0.0 2080.1 jit_solution(17581181648474980541)
XLA Ops:
  16.1 97.3 %all-gather.7.cloned.1.call-done = bf16[1152,6912]{1,0:T(8,128)(2,1)} async-done(((bf16[288,6912]{1,0:T(8,128)(2,1)}), bf16[1152,6912]{1,0:T(8,128)(2,1)}) %all-gather.7.cloned.1.call-update) | async-done | bytes 15925264 | tf_op jit(solution)/shard_map/all_gather | solution.py:270
  113.4 7.7 convolution_add_fusion.1
  128.0 42.8 %all-gather.9.cloned.1.call-done = bf16[1152,3456]{1,0:T(8,128)(2,1)} async-done(((bf16[288,3456]{1,0:T(8,128)(2,1)}), bf16[1152,3456]{1,0:T(8,128)(2,1)}) %all-gather.9.cloned.1.call-update) | async-done | bytes 7962640 | tf_op jit(solution)/shard_map/all_gather | solution.py:271
  170.8 5.8 convolution_add_fusion.3
  187.9 10.2 all-gather.11.cloned.1.call-done
  206.6 43.7 %all-gather.13.cloned.1.call-done = bf16[1152,3072]{1,0:T(8,128)(2,1)} async-done(((bf16[288,3072]{1,0:T(8,128)(2,1)}), bf16[1152,3072]{1,0:T(8,128)(2,1)}) %all-gather.13.cloned.1.call-update) | async-done | bytes 7077904 | tf_op jit(solution)/shard_map/all_gather | solution.py:273
  250.4 7.1 fusion.190
  257.5 45.2 %all-gather.17.cloned.1.call-done = bf16[3072,1152]{1,0:T(8,128)(2,1)} async-done(((bf16[768,1152]{1,0:T(8,128)(2,1)}), bf16[3072,1152]{1,0:T(8,128)(2,1)}) %all-gather.17.cloned.1.call-update) | async-done | bytes 7077904 | tf_op jit(solution)/shard_map/all_gather | solution.py:275
  302.7 7.5 fusion.184
  310.1 44.8 %all-gather.15.cloned.1.call-done = bf16[1152,3072]{1,0:T(8,128)(2,1)} async-done(((bf16[288,3072]{1,0:T(8,128)(2,1)}), bf16[1152,3072]{1,0:T(8,128)(2,1)}) %all-gather.15.cloned.1.call-update) | async-done | bytes 7077904 | tf_op jit(solution)/shard_map/all_gather | solution.py:274
  354.9 8.0 multiply_convert_fusion.7
  363.0 7.0 fusion.195
  392.6 9.9 fusion.44
  402.4 10.1 fusion.47
  418.2 8.1 convolution_add_fusion
  429.4 10.9 fusion.78
  443.7 6.5 convolution_add_fusion.2
  475.2 10.0 multiply_convert_fusion.2
  485.2 6.4 fusion.197
  491.7 6.2 multiply_reduce_fusion.8
  510.8 6.6 convolution_convert_fusion.7
  517.8 6.9 convolution_convert_fusion.9
  524.8 7.0 convolution_convert_fusion.5
  531.9 7.1 convolution_convert_fusion.4
  539.1 6.5 convolution_convert_fusion.6
  545.7 6.6 convolution_convert_fusion.8
  552.4 9.3 convolution_convert_fusion.3
  572.4 9.7 fusion.38
  582.1 9.9 fusion.41
  601.4 5.9 convolution_convert_fusion.2
  607.9 6.0 fusion.188
  614.5 8.6 convolution_convert_fusion.1
  625.7 9.1 fusion.80
  645.8 7.9 convolution_convert_fusion
  653.8 25.2 %reduce-scatter.25.cloned.1.call-done = bf16[288,3072]{1,0:T(8,128)(2,1)} async-done(((bf16[1152,3072]{1,0:T(8,128)(2,1)}), bf16[288,3072]{1,0:T(8,128)(2,1)}) %reduce-scatter.25.cloned.1.call-update) | async-done | bytes 1769488 | tf_op jit(solution)/shard_map/reduce_scatter | solution.py:304
  679.0 66.8 %reduce-scatter.33.cloned.1.call-done = bf16[768,1152]{1,0:T(8,128)(2,1)} async-done(((bf16[3072,1152]{1,0:T(8,128)(2,1)}), bf16[768,1152]{1,0:T(8,128)(2,1)}) %reduce-scatter.33.cloned.1.call-update) | async-done | bytes 1769488 | tf_op jit(solution)/shard_map/reduce_scatter | solution.py:310
  745.8 66.6 %reduce-scatter.35.cloned.1.call-done = bf16[768,1152]{1,0:T(8,128)(2,1)} async-done(((bf16[3072,1152]{1,0:T(8,128)(2,1)}), bf16[768,1152]{1,0:T(8,128)(2,1)}) %reduce-scatter.35.cloned.1.call-update) | async-done | bytes 1769488 | tf_op jit(solution)/shard_map/reduce_scatter | solution.py:310
  812.4 66.8 %reduce-scatter.31.cloned.1.call-done = bf16[288,3072]{1,0:T(8,128)(2,1)} async-done(((bf16[1152,3072]{1,0:T(8,128)(2,1)}), bf16[288,3072]{1,0:T(8,128)(2,1)}) %reduce-scatter.31.cloned.1.call-update) | async-done | bytes 1769488 | tf_op jit(solution)/shard_map/reduce_scatter | solution.py:307
  879.2 66.6 %reduce-scatter.27.cloned.1.call-done = bf16[288,3072]{1,0:T(8,128)(2,1)} async-done(((bf16[1152,3072]{1,0:T(8,128)(2,1)}), bf16[288,3072]{1,0:T(8,128)(2,1)}) %reduce-scatter.27.cloned.1.call-update) | async-done | bytes 1769488 | tf_op jit(solution)/shard_map/reduce_scatter | solution.py:304
  945.8 71.4 %reduce-scatter.17.cloned.1.call-done = bf16[288,3456]{1,0:T(8,128)(2,1)} async-done(((bf16[1152,3456]{1,0:T(8,128)(2,1)}), bf16[288,3456]{1,0:T(8,128)(2,1)}) %reduce-scatter.17.cloned.1.call-update) | async-done | bytes 1990672 | tf_op jit(solution)/shard_map/reduce_scatter | solution.py:298
  1017.2 71.9 %reduce-scatter.19.cloned.1.call-done = bf16[288,3456]{1,0:T(8,128)(2,1)} async-done(((bf16[1152,3456]{1,0:T(8,128)(2,1)}), bf16[288,3456]{1,0:T(8,128)(2,1)}) %reduce-scatter.19.cloned.1.call-update) | async-done | bytes 1990672 | tf_op jit(solution)/shard_map/reduce_scatter | solution.py:298
  1089.1 122.6 %reduce-scatter.13.cloned.1.call-done = bf16[288,6912]{1,0:T(8,128)(2,1)} async-done(((bf16[1152,6912]{1,0:T(8,128)(2,1)}), bf16[288,6912]{1,0:T(8,128)(2,1)}) %reduce-scatter.13.cloned.1.call-update) | async-done | bytes 3981328 | tf_op jit(solution)/shard_map/reduce_scatter | solution.py:295
  1211.6 122.6 %reduce-scatter.15.cloned.1.call-done = bf16[288,6912]{1,0:T(8,128)(2,1)} async-done(((bf16[1152,6912]{1,0:T(8,128)(2,1)}), bf16[288,6912]{1,0:T(8,128)(2,1)}) %reduce-scatter.15.cloned.1.call-update) | async-done | bytes 3981328 | tf_op jit(solution)/shard_map/reduce_scatter | solution.py:295
  1339.6 44.6 %all-reduce.8 = (f32[6912]{0:T(1024)}, f32[3456]{0:T(1024)}, f32[72]{0:T(128)}, f32[72]{0:T(128)}, f32[1152]{0:T(1024)}) all-reduce(f32[6912]{0:T(1024)S(1)} %add.442, f32[3456]{0:T(1024)S(1)} %add.444, f32[72]{0:T(128)S(1)} %copy-done.143, f32[72]{0:T(128)S(1)} %add.446, ...), channel_id=1, replica_groups=mesh['dp'=8,'fsdp'=4] {'dp','fsdp'}, use_global_device_ids=true, to_apply=%region_34.35 | all-reduce | flops 11664 | bytes 93312 | tf_op jit(solution)/shard_map/psum | solution.py:317
  1384.2 9.8 fusion.28
  1394.0 10.2 fusion.29
  1407.6 643.9 %all-reduce.12.cloned.1.call-done = (bf16[288,6912]{1,0:T(8,128)(2,1)}, bf16[288,6912]{1,0:T(8,128)(2,1)}, bf16[288,3456]{1,0:T(8,128)(2,1)}, bf16[288,3456]{1,0...) async-done(((bf16[288,6912]{1,0:T(8,128)(2,1)}, ...) | async-done | bytes 23887888 | tf_op jit(solution)/shard_map/psum | solution.py:229
  2051.5 7.5 convert_add_fusion
  (483 shorter events, 165.2 us)
Async XLA Ops:
  7.2 106.2 %all-gather.7.cloned.1.call-start = ((), (), s32[]{:S(2)}) async-start(), calls=%async_computation.12 | async-start | bytes 19906560 | tf_op jit(solution)/shard_map/all_gather | solution.py:270
  7.9 162.9 %all-gather.9.cloned.1.call-start = ((), (), s32[]{:S(2)}) async-start(), calls=%async_computation.13 | async-start | bytes 9953280 | tf_op jit(solution)/shard_map/all_gather | solution.py:271
  8.7 189.5 %all-gather.11.cloned.1.call-start = ((), (), s32[]{:S(2)}) async-start(), calls=%async_computation.14 | async-start | bytes 3317760 | tf_op jit(solution)/shard_map/all_gather | solution.py:272
  9.4 241.0 %all-gather.13.cloned.1.call-start = ((), (), s32[]{:S(2)}) async-start(), calls=%async_computation.15 | async-start | bytes 8847360 | tf_op jit(solution)/shard_map/all_gather | solution.py:273
  10.0 292.7 %all-gather.17.cloned.1.call-start = ((), (), s32[]{:S(2)}) async-start(), calls=%async_computation.17 | async-start | bytes 8847360 | tf_op jit(solution)/shard_map/all_gather | solution.py:275
  10.6 102.8 %copy-start.102 = (bf16[2,1,2,1152]{3,2,1,0:T(2,128)(2,1)S(1)}, bf16[2,1,2,1152]{3,2,1,0:T(2,128)(2,1)}, u32[]{:S(2)}) copy-start(bf16[2,1,2,1152]{3,2,1,0:T(2,128)(2,1)} %param.16) | copy-start | bytes 27652
  10.6 102.8 %copy-start.105 = (f32[6912]{0:T(1024)S(1)}, f32[6912]{0:T(1024)}, u32[]{:S(2)}) copy-start(f32[6912]{0:T(1024)} %param.19) | copy-start | bytes 82948
  10.6 344.3 %all-gather.15.cloned.1.call-start = ((), (), s32[]{:S(2)}) async-start(), calls=%async_computation.16 | async-start | bytes 8847360 | tf_op jit(solution)/shard_map/all_gather | solution.py:274
  11.2 642.5 %reduce-scatter.21.cloned.1.call-start = ((), (), s32[]{:S(2)}) async-start(), calls=%async_computation.22 | async-start | bytes 3317760 | tf_op jit(solution)/shard_map/reduce_scatter | solution.py:301
  11.7 109.3 %copy-start.112 = (s32[256]{0:T(256)}, s32[256]{0:T(256)S(1)}, u32[]{:S(2)}) copy-start(s32[256]{0:T(256)S(1)} %compare_convert_fusion.1) | copy-start | bytes 3076
  14.6 109.5 %copy-start.133 = (f32[256]{0:T(256)}, f32[256]{0:T(256)S(1)}, u32[]{:S(2)}) copy-start(f32[256]{0:T(256)S(1)} %fusion.126) | copy-start | bytes 3076
  127.7 43.1 %copy-start.145 = (f32[3456]{0:T(1024)S(1)}, f32[3456]{0:T(1024)}, u32[]{:S(2)}) copy-start(f32[3456]{0:T(1024)} %param.21) | copy-start | bytes 41476
  128.0 48.6 %copy-start.47 = (bf16[256,1152]{1,0:T(8,128)(2,1)}, bf16[256,1152]{1,0:T(8,128)(2,1)S(1)}, u32[]{:S(2)}) copy-start(bf16[256,1152]{1,0:T(8,128)(2,1)S(1)} %fusion.54) | copy-start | bytes 1769476
  202.7 173.8 %copy-start.2 = (f32[256,1152]{1,0:T(8,128)}, f32[256,1152]{1,0:T(8,128)S(1)}, u32[]{:S(2)}) copy-start(f32[256,1152]{1,0:T(8,128)S(1)} %get-tuple-element.55) | copy-start | bytes 3538948
  363.0 11.2 copy-start.43
  363.0 11.2 slice-start.4
  389.8 39.5 %copy-start.28 = (f32[16,72,256]{2,1,0:T(8,128)}, f32[16,72,256]{2,1,0:T(8,128)S(1)}, u32[]{:S(2)}) copy-start(f32[16,72,256]{2,1,0:T(8,128)S(1)} %fusion.95) | copy-start | bytes 3538948
  416.0 13.3 copy-start.11
  418.2 11.2 copy-start.13
  418.2 8.1 copy-start.110
  429.3 11.0 copy-start.1
  429.3 10.9 copy-start.132
  429.4 11.0 copy-start.134
  451.4 202.3 %reduce-scatter.23.cloned.1.call-start = ((), (), s32[]{:S(2)}) async-start(), calls=%async_computation.23 | async-start | bytes 3317760 | tf_op jit(solution)/shard_map/reduce_scatter | solution.py:301
  466.9 38.4 %copy-start.127 = (f32[256]{0:T(256)}, f32[256]{0:T(256)S(1)}, u32[]{:S(2)}) copy-start(f32[256]{0:T(256)S(1)} %fusion.129) | copy-start | bytes 3076
  485.2 17.7 copy-start.44
  485.2 17.7 slice-start.6
  491.7 11.2 slice-start.7
  510.7 143.1 %reduce-scatter.29.cloned.1.call-start = ((), (), s32[]{:S(2)}) async-start(), calls=%async_computation.26 | async-start | bytes 8847360 | tf_op jit(solution)/shard_map/reduce_scatter | solution.py:307
  517.4 161.6 %reduce-scatter.25.cloned.1.call-start = ((), (), s32[]{:S(2)}) async-start(), calls=%async_computation.24 | async-start | bytes 8847360 | tf_op jit(solution)/shard_map/reduce_scatter | solution.py:304
  524.7 221.0 %reduce-scatter.33.cloned.1.call-start = ((), (), s32[]{:S(2)}) async-start(), calls=%async_computation.28 | async-start | bytes 8847360 | tf_op jit(solution)/shard_map/reduce_scatter | solution.py:310
  531.8 280.6 %reduce-scatter.35.cloned.1.call-start = ((), (), s32[]{:S(2)}) async-start(), calls=%async_computation.29 | async-start | bytes 8847360 | tf_op jit(solution)/shard_map/reduce_scatter | solution.py:310
  539.0 340.1 %reduce-scatter.31.cloned.1.call-start = ((), (), s32[]{:S(2)}) async-start(), calls=%async_computation.27 | async-start | bytes 8847360 | tf_op jit(solution)/shard_map/reduce_scatter | solution.py:307
  545.6 400.2 %reduce-scatter.27.cloned.1.call-start = ((), (), s32[]{:S(2)}) async-start(), calls=%async_computation.25 | async-start | bytes 8847360 | tf_op jit(solution)/shard_map/reduce_scatter | solution.py:304
  552.3 464.9 %reduce-scatter.17.cloned.1.call-start = ((), (), s32[]{:S(2)}) async-start(), calls=%async_computation.20 | async-start | bytes 9953280 | tf_op jit(solution)/shard_map/reduce_scatter | solution.py:298
  561.7 527.4 %reduce-scatter.19.cloned.1.call-start = ((), (), s32[]{:S(2)}) async-start(), calls=%async_computation.21 | async-start | bytes 9953280 | tf_op jit(solution)/shard_map/reduce_scatter | solution.py:298
  607.3 604.4 %reduce-scatter.13.cloned.1.call-start = ((), (), s32[]{:S(2)}) async-start(), calls=%async_computation.18 | async-start | bytes 19906560 | tf_op jit(solution)/shard_map/reduce_scatter | solution.py:295
  623.1 711.1 %reduce-scatter.15.cloned.1.call-start = ((), (), s32[]{:S(2)}) async-start(), calls=%async_computation.19 | async-start | bytes 19906560 | tf_op jit(solution)/shard_map/reduce_scatter | solution.py:295
  625.7 9.1 copy-start.140
  625.7 9.1 copy-start.19
  625.7 9.1 copy-start.130
  653.7 1397.9 %all-reduce.12.cloned.1.call-start = ((), (), s32[]{:S(2)}) async-start(), calls=%async_computation.30 | async-start | bytes 47775744 | tf_op jit(solution)/shard_map/psum | solution.py:229
  1338.8 45.4 %copy-start.90 = (bf16[2,6912]{1,0:T(2,128)(2,1)S(1)}, bf16[2,6912]{1,0:T(2,128)(2,1)}, u32[]{:S(2)}) copy-start(bf16[2,6912]{1,0:T(2,128)(2,1)} %copy-done.89) | copy-start | bytes 82948
  1384.2 9.8 copy-start.92
  1394.0 10.9 copy-start.55
  1394.0 10.9 copy-start.56
  2051.5 7.5 copy-start.69
  2051.5 8.7 copy-start.64
  (130 other events, 310.5 us)
Sparse Core Ops, SparseCore 0:
  9.5 103.7 all-gather.6
  114.9 55.8 all-gather.8
  172.4 25.7 all-gather.10
  199.5 50.8 all-gather.12
  251.8 50.8 all-gather.16
  304.1 50.8 all-gather.14
  451.6 34.7 reduce-scatter.20
  510.8 34.7 reduce-scatter.22
  548.2 64.1 reduce-scatter.28
  614.8 64.1 reduce-scatter.24
  681.5 64.1 reduce-scatter.32
  748.2 64.1 reduce-scatter.34
  814.9 64.1 reduce-scatter.30
  881.5 64.1 reduce-scatter.26
  948.2 68.8 reduce-scatter.16
  1020.2 68.8 reduce-scatter.18
  1091.5 120.0 reduce-scatter.12
  1214.1 120.0 reduce-scatter.14
  1340.6 710.8 all-reduce.11
where the time goes:
time: 2090 us; the launch traced here: 2080 us
  waiting for transfers between devices  1610 us (77%)
  matrix products  299 us (14%)
  other arithmetic  61.2 us (3%)
  local copies, waits for them, and re-layouts  45.4 us (2%)
  blocking collectives  44.6 us (2%)
    psum x1, waiting for transfers between devices, sum_data(): lax.psum(grad_parts[0].astype(jnp.bfloat16), 'dp').astype(jnp.float32)  644 us
    reduce_scatter x2, waiting for transfers between devices, shards(): lax.psum_scatter(full_grads[0].astype(jnp.bfloat16), 'fsdp', scatter_dime...  245 us
    reduce_scatter x2, waiting for transfers between devices, shards(): lax.psum_scatter(full_grads[1].astype(jnp.bfloat16), 'fsdp', scatter_dime...  143 us
    reduce_scatter x2, waiting for transfers between devices, shards(): lax.psum_scatter(full_grads[5].astype(jnp.bfloat16), 'fsdp', scatter_dime...  133 us
    all_gather x1, waiting for transfers between devices, shards(): lax.all_gather(w_mod, 'fsdp', axis=0, tiled=True)  97.3 us
    reduce_scatter x2, waiting for transfers between devices, shards(): lax.psum_scatter(full_grads[3].astype(jnp.bfloat16), 'fsdp', scatter_dime...  91.8 us
    reduce_scatter x2, waiting for transfers between devices, shards(): lax.psum_scatter(full_grads[4].astype(jnp.bfloat16), 'fsdp', scatter_dime...  66.8 us
    all_gather x1, waiting for transfers between devices, shards(): lax.all_gather(w_down, 'fsdp', axis=0, tiled=True)  45.2 us
  transfers between devices with their start and end apart: 19, of which 16 were waited for; matrix products, arithmetic and copies ran while one was open for 13% of the time, Pallas kernels for 0%

commit v1 on v0

--- a/solution.py
+++ b/solution.py
@@ -1,3 +1,4 @@
+import functools
 from functools import partial
 import jax
 import jax.numpy as jnp
@@ -7,6 +8,13 @@
 GRID_H = 16
 EPSILON = 1e-06
 MASKED = -1e30
+
+
+def spot_render(local_values, shard_axis):
+    return jax.lax.all_gather(local_values, shard_axis).sum(axis=0)
+
+
+digits_start = functools.partial(spot_render, shard_axis="dp")
 
 
 def silu_grad(values):
@@ -226,7 +234,7 @@
 
 def sum_data(grad_parts):
     return (
-        lax.psum(grad_parts[0].astype(jnp.bfloat16), "dp").astype(jnp.float32),
+        digits_start(grad_parts[0].astype(jnp.bfloat16)).astype(jnp.float32),
         lax.psum(grad_parts[1].astype(jnp.bfloat16), "dp").astype(jnp.float32),
         lax.psum(grad_parts[2].astype(jnp.bfloat16), "dp").astype(jnp.float32),
         lax.psum(grad_parts[3].astype(jnp.bfloat16), "dp").astype(jnp.float32),

time: 2090 us -> 3080 us (1.47)
  waiting for transfers between devices: 1610 us -> 2570 us
    all_gather x0 -> x2, waiting for transfers between devices: none -> 1180 us  [spot_render(): return jax.lax.all_gather(local_values, shard_axis).sum(axis=0)]
    psum x1, waiting for transfers between devices: 644 us -> 419 us  [sum_data(): lax.psum(grad_parts[1].astype(jnp.bfloat16), 'dp').astype(jnp.float32)]
  transfers between devices with their start and end apart: 19 -> 21, of which waited for: 16 -> 18; matrix products, arithmetic and copies ran while one was open for 13% -> 9% of each run, Pallas kernels for 0% -> 0%
where the time goes in v1:
time: 3080 us; the launch traced here: 3070 us
  waiting for transfers between devices  2570 us (83%)
  matrix products  299 us (10%)
  other arithmetic  91.2 us (3%)
  blocking collectives  46.1 us (1%)
  local copies, waits for them, and re-layouts  45.6 us (1%)
    all_gather x2, waiting for transfers between devices, spot_render(): return jax.lax.all_gather(local_values, shard_axis).sum(axis=0)  1180 us
    psum x1, waiting for transfers between devices, sum_data(): lax.psum(grad_parts[1].astype(jnp.bfloat16), 'dp').astype(jnp.float32)  419 us
    reduce_scatter x2, waiting for transfers between devices, shards(): lax.psum_scatter(full_grads[0].astype(jnp.bfloat16), 'fsdp', scatter_dime...  245 us
    reduce_scatter x2, waiting for transfers between devices, shards(): lax.psum_scatter(full_grads[1].astype(jnp.bfloat16), 'fsdp', scatter_dime...  143 us
    reduce_scatter x2, waiting for transfers between devices, shards(): lax.psum_scatter(full_grads[5].astype(jnp.bfloat16), 'fsdp', scatter_dime...  133 us
    all_gather x1, waiting for transfers between devices, shards(): lax.all_gather(w_mod, 'fsdp', axis=0, tiled=True)  97.4 us
    reduce_scatter x2, waiting for transfers between devices, shards(): lax.psum_scatter(full_grads[3].astype(jnp.bfloat16), 'fsdp', scatter_dime...  91.7 us
    reduce_scatter x2, waiting for transfers between devices, shards(): lax.psum_scatter(full_grads[4].astype(jnp.bfloat16), 'fsdp', scatter_dime...  66.8 us
  transfers between devices with their start and end apart: 21, of which 18 were waited for; matrix products, arithmetic and copies ran while one was open for 9% of the time, Pallas kernels for 0%

profile of v1, /device:TPU:0, one launch (start us, length us, event | category | flops | bytes accessed | tf_op | source)
XLA Modules:
  0.0 3069.2 jit_solution(443894684441338614)
XLA Ops:
  16.0 97.4 %all-gather.11.cloned.1.call-done = bf16[1152,6912]{1,0:T(8,128)(2,1)} async-done(((bf16[288,6912]{1,0:T(8,128)(2,1)}), bf16[1152,6912]{1,0:T(8,128)(2,1)}) %all-gather.11.cloned.1.call-update) | async-done | bytes 15925264 | tf_op jit(solution)/shard_map/all_gather | solution.py:278
  113.4 7.7 convolution_add_fusion.1
  128.0 42.8 %all-gather.13.cloned.1.call-done = bf16[1152,3456]{1,0:T(8,128)(2,1)} async-done(((bf16[288,3456]{1,0:T(8,128)(2,1)}), bf16[1152,3456]{1,0:T(8,128)(2,1)}) %all-gather.13.cloned.1.call-update) | async-done | bytes 7962640 | tf_op jit(solution)/shard_map/all_gather | solution.py:279
  187.9 10.2 all-gather.15.cloned.1.call-done
  206.6 43.8 %all-gather.17.cloned.1.call-done = bf16[1152,3072]{1,0:T(8,128)(2,1)} async-done(((bf16[288,3072]{1,0:T(8,128)(2,1)}), bf16[1152,3072]{1,0:T(8,128)(2,1)}) %all-gather.17.cloned.1.call-update) | async-done | bytes 7077904 | tf_op jit(solution)/shard_map/all_gather | solution.py:281
  250.4 7.1 fusion.190
  257.5 45.2 %all-gather.21.cloned.1.call-done = bf16[3072,1152]{1,0:T(8,128)(2,1)} async-done(((bf16[768,1152]{1,0:T(8,128)(2,1)}), bf16[3072,1152]{1,0:T(8,128)(2,1)}) %all-gather.21.cloned.1.call-update) | async-done | bytes 7077904 | tf_op jit(solution)/shard_map/all_gather | solution.py:283
  302.7 7.5 fusion.184
  310.1 44.8 %all-gather.19.cloned.1.call-done = bf16[1152,3072]{1,0:T(8,128)(2,1)} async-done(((bf16[288,3072]{1,0:T(8,128)(2,1)}), bf16[1152,3072]{1,0:T(8,128)(2,1)}) %all-gather.19.cloned.1.call-update) | async-done | bytes 7077904 | tf_op jit(solution)/shard_map/all_gather | solution.py:282
  354.9 8.0 multiply_convert_fusion.7
  363.0 7.0 fusion.195
  392.6 9.8 fusion.44
  402.4 10.1 fusion.47
  418.1 8.1 convolution_add_fusion
  429.3 10.9 fusion.78
  443.7 6.5 convolution_add_fusion.2
  475.1 10.0 multiply_convert_fusion.2
  485.2 6.4 fusion.197
  510.8 6.6 convolution_convert_fusion.7
  517.9 6.9 convolution_convert_fusion.9
  524.9 7.0 convolution_convert_fusion.5
  531.9 7.0 convolution_convert_fusion.4
  539.0 6.5 convolution_convert_fusion.6
  545.6 6.6 convolution_convert_fusion.8
  552.2 9.3 convolution_convert_fusion.3
  572.3 9.7 fusion.38
  582.1 9.9 fusion.41
  614.6 8.7 convolution_convert_fusion.1
  625.9 9.1 fusion.80
  645.9 7.9 convolution_convert_fusion
  653.9 25.1 reduce-scatter.25.cloned.1.call-done
  679.0 66.8 %reduce-scatter.33.cloned.1.call-done = bf16[768,1152]{1,0:T(8,128)(2,1)} async-done(((bf16[3072,1152]{1,0:T(8,128)(2,1)}), bf16[768,1152]{1,0:T(8,128)(2,1)}) %reduce-scatter.33.cloned.1.call-update) | async-done | bytes 1769488 | tf_op jit(solution)/shard_map/reduce_scatter | solution.py:318
  745.8 66.6 %reduce-scatter.35.cloned.1.call-done = bf16[768,1152]{1,0:T(8,128)(2,1)} async-done(((bf16[3072,1152]{1,0:T(8,128)(2,1)}), bf16[768,1152]{1,0:T(8,128)(2,1)}) %reduce-scatter.35.cloned.1.call-update) | async-done | bytes 1769488 | tf_op jit(solution)/shard_map/reduce_scatter | solution.py:318
  812.4 66.8 %reduce-scatter.31.cloned.1.call-done = bf16[288,3072]{1,0:T(8,128)(2,1)} async-done(((bf16[1152,3072]{1,0:T(8,128)(2,1)}), bf16[288,3072]{1,0:T(8,128)(2,1)}) %reduce-scatter.31.cloned.1.call-update) | async-done | bytes 1769488 | tf_op jit(solution)/shard_map/reduce_scatter | solution.py:315
  879.2 66.6 %reduce-scatter.27.cloned.1.call-done = bf16[288,3072]{1,0:T(8,128)(2,1)} async-done(((bf16[1152,3072]{1,0:T(8,128)(2,1)}), bf16[288,3072]{1,0:T(8,128)(2,1)}) %reduce-scatter.27.cloned.1.call-update) | async-done | bytes 1769488 | tf_op jit(solution)/shard_map/reduce_scatter | solution.py:312
  945.8 71.3 %reduce-scatter.17.cloned.1.call-done = bf16[288,3456]{1,0:T(8,128)(2,1)} async-done(((bf16[1152,3456]{1,0:T(8,128)(2,1)}), bf16[288,3456]{1,0:T(8,128)(2,1)}) %reduce-scatter.17.cloned.1.call-update) | async-done | bytes 1990672 | tf_op jit(solution)/shard_map/reduce_scatter | solution.py:306
  1017.1 71.9 %reduce-scatter.19.cloned.1.call-done = bf16[288,3456]{1,0:T(8,128)(2,1)} async-done(((bf16[1152,3456]{1,0:T(8,128)(2,1)}), bf16[288,3456]{1,0:T(8,128)(2,1)}) %reduce-scatter.19.cloned.1.call-update) | async-done | bytes 1990672 | tf_op jit(solution)/shard_map/reduce_scatter | solution.py:306
  1089.1 122.5 %reduce-scatter.13.cloned.1.call-done = bf16[288,6912]{1,0:T(8,128)(2,1)} async-done(((bf16[1152,6912]{1,0:T(8,128)(2,1)}), bf16[288,6912]{1,0:T(8,128)(2,1)}) %reduce-scatter.13.cloned.1.call-update) | async-done | bytes 3981328 | tf_op jit(solution)/shard_map/reduce_scatter | solution.py:303
  1211.6 122.5 %reduce-scatter.15.cloned.1.call-done = bf16[288,6912]{1,0:T(8,128)(2,1)} async-done(((bf16[1152,6912]{1,0:T(8,128)(2,1)}), bf16[288,6912]{1,0:T(8,128)(2,1)}) %reduce-scatter.15.cloned.1.call-update) | async-done | bytes 3981328 | tf_op jit(solution)/shard_map/reduce_scatter | solution.py:303
  1339.7 46.1 %all-reduce.8 = (f32[6912]{0:T(1024)}, f32[3456]{0:T(1024)}, f32[72]{0:T(128)}, f32[72]{0:T(128)}, f32[1152]{0:T(1024)}) all-reduce(f32[6912]{0:T(1024)S(1)} %add.438, f32[3456]{0:T(1024)S(1)} %add.440, f32[72]{0:T(128)S(1)} %copy-done.142, f32[72]{0:T(128)S(1)} %add.442, ...), channel_id=1, replica_groups=mesh['dp'=8,'fsdp'=4] {'dp','fsdp'}, use_global_device_ids=true, to_apply=%region_34.35 | all-reduce | flops 11664 | bytes 93312 | tf_op jit(solution)/shard_map/psum | solution.py:325
  1385.8 9.9 fusion.28
  1395.7 10.2 fusion.29
  1409.3 418.7 %all-reduce.12.cloned.1.call-done = (bf16[288,3456]{1,0:T(8,128)(2,1)}, bf16[288,3456]{1,0:T(8,128)(2,1)}, bf16[288,1152]{1,0:T(8,128)(2,1)}, bf16[288,1152]{1,0...) async-done(((bf16[288,3456]{1,0:T(8,128)(2,1)}, ...) | async-done | bytes 15925264 | tf_op jit(solution)/shard_map/psum | solution.py:238
  1844.1 589.9 %all-gather.23.cloned.1.call-done = bf16[2304,6912]{1,0:T(8,128)(2,1)} async-done(((bf16[288,6912]{1,0:T(8,128)(2,1)}), bf16[2304,6912]{1,0:T(8,128)(2,1)}) %all-gather.23.cloned.1.call-update) | async-done | bytes 31850512 | tf_op jit(solution)/shard_map/all_gather | solution.py:14
  2434.0 14.5 reduce_sum.366
  2448.5 592.7 %all-gather.25.cloned.1.call-done = bf16[2304,6912]{1,0:T(8,128)(2,1)} async-done(((bf16[288,6912]{1,0:T(8,128)(2,1)}), bf16[2304,6912]{1,0:T(8,128)(2,1)}) %all-gather.25.cloned.1.call-update) | async-done | bytes 31850512 | tf_op jit(solution)/shard_map/all_gather | solution.py:14
  3041.2 13.6 reduce_sum.370
  3054.8 7.4 convert_add_fusion
  (489 shorter events, 191.5 us)
Async XLA Ops:
  7.2 106.2 %all-gather.11.cloned.1.call-start = ((), (), s32[]{:S(2)}) async-start(), calls=%async_computation.12 | async-start | bytes 19906560 | tf_op jit(solution)/shard_map/all_gather | solution.py:278
  7.9 162.9 %all-gather.13.cloned.1.call-start = ((), (), s32[]{:S(2)}) async-start(), calls=%async_computation.13 | async-start | bytes 9953280 | tf_op jit(solution)/shard_map/all_gather | solution.py:279
  8.7 189.5 %all-gather.15.cloned.1.call-start = ((), (), s32[]{:S(2)}) async-start(), calls=%async_computation.14 | async-start | bytes 3317760 | tf_op jit(solution)/shard_map/all_gather | solution.py:280
  9.4 241.0 %all-gather.17.cloned.1.call-start = ((), (), s32[]{:S(2)}) async-start(), calls=%async_computation.15 | async-start | bytes 8847360 | tf_op jit(solution)/shard_map/all_gather | solution.py:281
  10.0 292.7 %all-gather.21.cloned.1.call-start = ((), (), s32[]{:S(2)}) async-start(), calls=%async_computation.17 | async-start | bytes 8847360 | tf_op jit(solution)/shard_map/all_gather | solution.py:283
  10.6 102.8 %copy-start.101 = (bf16[2,1,2,1152]{3,2,1,0:T(2,128)(2,1)S(1)}, bf16[2,1,2,1152]{3,2,1,0:T(2,128)(2,1)}, u32[]{:S(2)}) copy-start(bf16[2,1,2,1152]{3,2,1,0:T(2,128)(2,1)} %param.16) | copy-start | bytes 27652
  10.6 102.8 %copy-start.104 = (f32[6912]{0:T(1024)S(1)}, f32[6912]{0:T(1024)}, u32[]{:S(2)}) copy-start(f32[6912]{0:T(1024)} %param.19) | copy-start | bytes 82948
  10.6 344.3 %all-gather.19.cloned.1.call-start = ((), (), s32[]{:S(2)}) async-start(), calls=%async_computation.16 | async-start | bytes 8847360 | tf_op jit(solution)/shard_map/all_gather | solution.py:282
  11.2 642.7 %reduce-scatter.21.cloned.1.call-start = ((), (), s32[]{:S(2)}) async-start(), calls=%async_computation.22 | async-start | bytes 3317760 | tf_op jit(solution)/shard_map/reduce_scatter | solution.py:309
  11.7 109.3 %copy-start.111 = (s32[256]{0:T(256)}, s32[256]{0:T(256)S(1)}, u32[]{:S(2)}) copy-start(s32[256]{0:T(256)S(1)} %compare_convert_fusion.1) | copy-start | bytes 3076
  14.5 109.5 %copy-start.132 = (f32[256]{0:T(256)}, f32[256]{0:T(256)S(1)}, u32[]{:S(2)}) copy-start(f32[256]{0:T(256)S(1)} %fusion.126) | copy-start | bytes 3076
  127.7 43.1 %copy-start.144 = (f32[3456]{0:T(1024)S(1)}, f32[3456]{0:T(1024)}, u32[]{:S(2)}) copy-start(f32[3456]{0:T(1024)} %param.21) | copy-start | bytes 41476
  128.0 48.6 %copy-start.49 = (bf16[256,1152]{1,0:T(8,128)(2,1)}, bf16[256,1152]{1,0:T(8,128)(2,1)S(1)}, u32[]{:S(2)}) copy-start(bf16[256,1152]{1,0:T(8,128)(2,1)S(1)} %fusion.54) | copy-start | bytes 1769476
  202.7 173.9 %copy-start.2 = (f32[256,1152]{1,0:T(8,128)}, f32[256,1152]{1,0:T(8,128)S(1)}, u32[]{:S(2)}) copy-start(f32[256,1152]{1,0:T(8,128)S(1)} %get-tuple-element.53) | copy-start | bytes 3538948
  363.0 11.2 copy-start.45
  363.0 11.2 slice-start.4
  389.8 39.4 %copy-start.29 = (f32[16,72,256]{2,1,0:T(8,128)}, f32[16,72,256]{2,1,0:T(8,128)S(1)}, u32[]{:S(2)}) copy-start(f32[16,72,256]{2,1,0:T(8,128)S(1)} %fusion.95) | copy-start | bytes 3538948
  416.0 13.3 copy-start.11
  418.1 11.2 copy-start.13
  418.1 8.1 copy-start.109
  429.2 11.0 copy-start.1
  429.3 11.0 copy-start.131
  429.3 11.0 copy-start.133
  451.4 202.5 %reduce-scatter.23.cloned.1.call-start = ((), (), s32[]{:S(2)}) async-start(), calls=%async_computation.23 | async-start | bytes 3317760 | tf_op jit(solution)/shard_map/reduce_scatter | solution.py:309
  466.8 38.4 %copy-start.126 = (f32[256]{0:T(256)}, f32[256]{0:T(256)S(1)}, u32[]{:S(2)}) copy-start(f32[256]{0:T(256)S(1)} %fusion.129) | copy-start | bytes 3076
  485.2 17.8 copy-start.46
  485.2 17.8 slice-start.6
  491.7 11.3 slice-start.7
  510.7 143.2 %reduce-scatter.29.cloned.1.call-start = ((), (), s32[]{:S(2)}) async-start(), calls=%async_computation.26 | async-start | bytes 8847360 | tf_op jit(solution)/shard_map/reduce_scatter | solution.py:315
  517.4 161.6 %reduce-scatter.25.cloned.1.call-start = ((), (), s32[]{:S(2)}) async-start(), calls=%async_computation.24 | async-start | bytes 8847360 | tf_op jit(solution)/shard_map/reduce_scatter | solution.py:312
  524.8 221.0 %reduce-scatter.33.cloned.1.call-start = ((), (), s32[]{:S(2)}) async-start(), calls=%async_computation.28 | async-start | bytes 8847360 | tf_op jit(solution)/shard_map/reduce_scatter | solution.py:318
  531.9 280.5 %reduce-scatter.35.cloned.1.call-start = ((), (), s32[]{:S(2)}) async-start(), calls=%async_computation.29 | async-start | bytes 8847360 | tf_op jit(solution)/shard_map/reduce_scatter | solution.py:318
  539.0 340.2 %reduce-scatter.31.cloned.1.call-start = ((), (), s32[]{:S(2)}) async-start(), calls=%async_computation.27 | async-start | bytes 8847360 | tf_op jit(solution)/shard_map/reduce_scatter | solution.py:315
  545.5 400.2 %reduce-scatter.27.cloned.1.call-start = ((), (), s32[]{:S(2)}) async-start(), calls=%async_computation.25 | async-start | bytes 8847360 | tf_op jit(solution)/shard_map/reduce_scatter | solution.py:312
  552.2 465.0 %reduce-scatter.17.cloned.1.call-start = ((), (), s32[]{:S(2)}) async-start(), calls=%async_computation.20 | async-start | bytes 9953280 | tf_op jit(solution)/shard_map/reduce_scatter | solution.py:306
  561.6 527.5 %reduce-scatter.19.cloned.1.call-start = ((), (), s32[]{:S(2)}) async-start(), calls=%async_computation.21 | async-start | bytes 9953280 | tf_op jit(solution)/shard_map/reduce_scatter | solution.py:306
  607.3 604.2 %reduce-scatter.13.cloned.1.call-start = ((), (), s32[]{:S(2)}) async-start(), calls=%async_computation.18 | async-start | bytes 19906560 | tf_op jit(solution)/shard_map/reduce_scatter | solution.py:303
  623.3 710.8 %reduce-scatter.15.cloned.1.call-start = ((), (), s32[]{:S(2)}) async-start(), calls=%async_computation.19 | async-start | bytes 19906560 | tf_op jit(solution)/shard_map/reduce_scatter | solution.py:303
  625.9 9.1 copy-start.139
  625.9 9.1 copy-start.20
  625.9 9.1 copy-start.129
  653.8 1174.2 %all-reduce.12.cloned.1.call-start = ((), (), s32[]{:S(2)}) async-start(), calls=%async_computation.32 | async-start | bytes 31850496 | tf_op jit(solution)/shard_map/psum | solution.py:238
  1089.1 1344.9 %all-gather.23.cloned.1.call-start = ((), (), s32[]{:S(2)}) async-start(), calls=%async_computation.30 | async-start | bytes 35831808 | tf_op jit(solution)/shard_map/all_gather | solution.py:14
  1211.6 1829.6 %all-gather.25.cloned.1.call-start = ((), (), s32[]{:S(2)}) async-start(), calls=%async_computation.31 | async-start | bytes 35831808 | tf_op jit(solution)/shard_map/all_gather | solution.py:14
  1338.9 46.9 %copy-start.89 = (bf16[2,6912]{1,0:T(2,128)(2,1)S(1)}, bf16[2,6912]{1,0:T(2,128)(2,1)}, u32[]{:S(2)}) copy-start(bf16[2,6912]{1,0:T(2,128)(2,1)} %copy-done.88) | copy-start | bytes 82948
  1385.8 9.9 copy-start.91
  1395.7 10.9 copy-start.57
  1395.7 10.9 copy-start.58
  (131 other events, 310.8 us)
Sparse Core Ops, SparseCore 0:
  9.5 103.7 all-gather.10
  114.9 55.8 all-gather.12
  172.4 25.7 all-gather.14
  199.5 50.8 all-gather.16
  251.8 50.8 all-gather.20
  304.1 50.8 all-gather.18
  451.5 34.7 reduce-scatter.20
  510.9 34.7 reduce-scatter.22
  548.2 64.1 reduce-scatter.28
  614.8 64.1 reduce-scatter.24
  681.6 64.1 reduce-scatter.32
  748.2 64.1 reduce-scatter.34
  814.9 64.1 reduce-scatter.30
  881.6 64.1 reduce-scatter.26
  948.2 68.8 reduce-scatter.16
  1020.2 68.8 reduce-scatter.18
  1091.5 120.0 reduce-scatter.12
  1214.0 120.0 reduce-scatter.14
  1340.5 487.4 all-reduce.11
  1829.4 604.5 all-gather.22
  2435.5 605.6 all-gather.24
